TPU v7x, 32 devices: a whole 2x2x4 slice. The times are simulated.
32 devices in a mesh: seq: 16 (over z, y, core), head: 2 (over x).
Axes of the slice: x: 2, y: 2, z: 4, core: 2. Of those that a mesh axis runs over, the one named last changes fastest.
Arguments:
- tokens: bfloat16 [8192, 5120], P(('seq', 'head')), may hold values from -6 to 6
- w_qkv: bfloat16 [3, 5120, 640], P(None, None, 'head'), may hold values from -0.078125 to 0.078125
- scale_exp: int32 [3, 40, 2], P(None, None, 'head'), may hold values from -2 to 1
- gate_mask: int32 [8192, 2], P('seq', 'head'), may hold values 0 or 1
- rate: float32 [2], P('head'), may hold values from 0.00044194172 to 0.0022097088
- fast_gate: bfloat16 [2, 320, 640], P('head'), may hold values from -0.3125 to 0.3125
- fast_up: bfloat16 [2, 320, 640], P('head'), may hold values from -0.3125 to 0.3125
- fast_down: bfloat16 [2, 320, 640], P('head'), may hold values from -0.25 to 0.25
Outputs:
- answers: bfloat16 [8192, 640], P(('seq', 'head'))
All inputs are finite; a program needn't handle non-finite values. No bound on the sum of `gate_mask` on one device may be relied on, other than what follows from the above.
Results may differ from a plain program's by a relative error of at most 0.012.
Values may be sent and summed in bfloat16 or wider, within the bound.
A program may use at most 64 MiB of HBM per device.

v0:
```python
import jax
import jax.numpy as jnp
from jax import lax
from jax.sharding import PartitionSpec as P


def local_grads(keys, values, weight, old):
    gate = jnp.dot(keys, old[0], preferred_element_type=jnp.float32)
    upper = jnp.dot(keys, old[1], preferred_element_type=jnp.float32)
    sigma = jax.nn.sigmoid(gate)
    active = gate * sigma
    hidden = (active * upper).astype(jnp.bfloat16)
    weighted = (weight[:, None] * values.astype(jnp.float32)).astype(jnp.bfloat16)
    d_hidden = jnp.dot(weighted, old[2], preferred_element_type=jnp.float32)
    d_gate = (d_hidden * upper * sigma * (1.0 + gate * (1.0 - sigma))).astype(jnp.bfloat16)
    d_upper = (d_hidden * active).astype(jnp.bfloat16)
    dims = (((0,), (0,)), ((), ()))
    grad_gate = lax.dot_general(keys, d_gate, dims, preferred_element_type=jnp.float32)
    grad_upper = lax.dot_general(keys, d_upper, dims, preferred_element_type=jnp.float32)
    grad_down = lax.dot_general(weighted, hidden, dims, preferred_element_type=jnp.float32)
    return jnp.stack([grad_gate, grad_upper, grad_down])


def respond(query, renorm):
    gate = jnp.dot(query, renorm[0], preferred_element_type=jnp.float32)
    upper = jnp.dot(query, renorm[1], preferred_element_type=jnp.float32)
    hidden = (jax.nn.silu(gate) * upper).astype(jnp.bfloat16)
    output = lax.dot_general(
        hidden, renorm[2], (((1,), (1,)), ((), ())), preferred_element_type=jnp.float32
    )
    scaled = output * lax.rsqrt(jnp.mean(output * output, axis=-1, keepdims=True) + 1e-05)
    return scaled.astype(jnp.bfloat16)


def body(tokens, w_qkv, scale_exp, gate_mask, rate, fast_gate, fast_up, fast_down):
    factor = jnp.exp2(scale_exp.astype(jnp.float32))[:, :, 0]
    block_rows = w_qkv.shape[1] // factor.shape[1]
    factor = jnp.repeat(factor, block_rows, axis=1)[:, :, None].astype(jnp.bfloat16)
    weff = w_qkv * factor
    triple = jnp.einsum(
        "rd,cdh->rch",
        lax.all_gather(tokens, "head", axis=0, tiled=True),
        weff,
        preferred_element_type=jnp.float32,
    ).astype(jnp.bfloat16)
    query = triple[:, 0]
    keys = triple[:, 1]
    values = triple[:, 2]
    weight = rate[0] * gate_mask[:, 0].astype(jnp.float32)
    old = jnp.stack([fast_gate[0], fast_up[0], fast_down[0]])
    partial_grads = local_grads(keys, values, weight, old)
    old_f = old.astype(jnp.float32)
    old_norm = jnp.sqrt(jnp.sum(old_f * old_f, axis=1))
    total = lax.psum(partial_grads, "seq")
    fresh = old_f + total
    new_sq = jnp.sum(fresh * fresh, axis=1)
    renorm = (fresh * (old_norm / jnp.sqrt(new_sq + 1e-06))[:, None, :]).astype(jnp.bfloat16)
    answer = respond(query, renorm)
    return lax.all_to_all(answer, "head", split_axis=0, concat_axis=1, tiled=True)


def solution(mesh):
    in_specs = (
        P(("seq", "head"), None),
        P(None, None, "head"),
        P(None, None, "head"),
        P("seq", "head"),
        P("head"),
        P("head", None, None),
        P("head", None, None),
        P("head", None, None),
    )
    out_specs = P(("seq", "head"), None)
    return jax.shard_map(body, mesh=mesh, in_specs=in_specs, out_specs=out_specs, check_vma=False)
```

profile of v0, /device:TPU:0, one launch (start us, length us, event | category | flops | bytes accessed | tf_op | source)
XLA Modules:
  0.0 218.8 jit_solution(169645211959964053)
XLA Ops:
  6.5 0.0 copy-start.5
  6.5 0.0 copy-start.4
  6.5 0.0 all-gather.2.cloned.1.call-start
  6.5 0.7 all-gather.2.cloned.1.call-update
  7.3 0.0 all-reduce.2.cloned.1.call-start
  8.0 0.0 copy-done.5
  8.0 0.1 broadcast_bitcast_fusion
  8.1 0.0 copy-done.4
  8.1 72.0 %all-gather.2.cloned.1.call-done = bf16[512,5120]{1,0:T(8,128)(2,1)} async-done(((bf16[256,5120]{1,0:T(8,128)(2,1)}), bf16[512,5120]{1,0:T(8,128)(2,1)}) %all-gather.2.cloned.1.call-update) | async-done | bytes 5242896 | tf_op jit(solution)/shard_map/all_gather | solution.py:42
  80.2 0.0 copy-start.2
  80.2 9.5 %fusion.10 = bf16[512,3,320]{0,2,1:T(8,128)(2,1)S(1)} fusion(bf16[512,5120]{1,0:T(8,128)(2,1)} %all-gather.2.cloned.1.call-done, bf16[3,5120,320]{1,2,0:T(8,128)(2,1)} %param.9, bf16[3,5120]{1,0:T(4,128)(2,1)S(1)} %bitcast.82), kind=kOutput, calls=%fused_computation.12 | convolution fusion | flops 5038571520 | bytes 16087040 | tf_op jit(solution)/shard_map/rd,cdh->rch/dot_general | solution.py:40
  89.7 0.0 copy-done.2
  89.7 0.0 copy-start.1
  89.7 0.6 fusion.23
  90.3 0.4 copy-done.1
  90.7 0.0 copy-start.3
  90.7 0.6 fusion.25
  91.3 0.4 copy-done.3
  91.7 0.6 fusion.27
  92.3 0.6 convolution_bitcast_fusion.1
  92.9 0.8 convolution_bitcast_fusion.2
  93.7 0.6 convolution_bitcast_fusion
  94.3 1.6 pad_maximum_fusion
  95.9 0.0 all-reduce.2.cloned.1.call-update
  96.0 100.3 %all-reduce.2.cloned.1.call-done = f32[3,320,640]{2,1,0:T(8,128)} async-done(((f32[3,320,640]{2,1,0:T(8,128)}), f32[3,320,640]{2,1,0:T(8,128)}) %all-reduce.2.cloned.1.call-update) | async-done | bytes 2457616 | tf_op jit(solution)/shard_map/psum | solution.py:54
  196.2 0.0 copy-start
  196.2 2.4 %fusion.4 = (f32[3,640]{1,0:T(4,128)S(1)}, f32[3,640]{1,0:T(4,128)S(1)}) fusion(bf16[1,320,640]{2,1,0:T(8,128)(2,1)S(1)} %copy-done.3, bf16[1,320,640]{2,1,0:T(8,128)(2,1)S(1)} %copy-done.1, bf16[1,320,640]{2,1,0:T(8,128)(2,1)S(1)} %copy-done.2, f32[3,320,640]{2,1,0:T(8,128)} %all-reduce.2.cloned.1.call-done), kind=kLoop, calls=%fused_computation.6 | loop fusion | flops 4911360 | bytes 3701760 | tf_op jit(solution)/shard_map/reduce_sum | solution.py:53
  198.6 0.1 copy-done
  198.7 0.4 multiply_convert_fusion
  199.0 1.6 fusion.22
  200.7 2.3 %multiply_reduce_fusion.1 = (f32[512]{0:T(512)S(1)}, f32[512,320]{0,1:T(8,128)S(1)}) fusion(bf16[3,320,640]{2,1,0:T(8,128)(2,1)S(1)} %multiply_convert_fusion, f32[512,640]{1,0:T(8,128)} %fusion.22, bf16[512,3,320]{0,2,1:T(8,128)(2,1)S(1)} %fusion.10), kind=kOutput, calls=%fused_computation.30 | convolution fusion | flops 421723648 | bytes 3115008 | tf_op jit(solution)/shard_map/dot_general | solution.py:28
  203.0 0.1 multiply_convert_fusion.6
  203.1 7.9 %all_to_all.19 = bf16[2,256,320]{1,2,0:T(8,128)(2,1)S(1)} all-to-all(bf16[2,256,320]{1,2,0:T(8,128)(2,1)S(1)} %bitcast.79), channel_id=1, replica_groups=mesh['seq'=16,'head'=2] {'head'}, dimensions={0} | all-to-all | bytes 655360 | tf_op jit(solution)/shard_map/all_to_all | solution.py:59
  211.1 0.9 copy.11
  (7 shorter events, 0.1 us)
Async XLA Ops:
  6.5 1.4 copy-start.5
  6.5 1.6 copy-start.4
  6.5 73.6 %all-gather.2.cloned.1.call-start = ((), (), s32[]{:S(2)}) async-start(), calls=%async_computation.1 | async-start | bytes 7864320 | tf_op jit(solution)/shard_map/all_gather | solution.py:42
  7.3 189.0 %all-reduce.2.cloned.1.call-start = ((), (), s32[]{:S(2)}) async-start(), calls=%async_computation.2 | async-start | bytes 4915200 | tf_op jit(solution)/shard_map/psum | solution.py:54
  80.2 9.5 %copy-start.2 = (bf16[1,320,640]{2,1,0:T(8,128)(2,1)S(1)}, bf16[1,320,640]{2,1,0:T(8,128)(2,1)}, u32[]{:S(2)}) copy-start(bf16[1,320,640]{2,1,0:T(8,128)(2,1)} %param.13) | copy-start | bytes 1228804
  89.7 1.0 copy-start.1
  90.7 1.0 copy-start.3
  196.2 2.4 %copy-start = (f32[3,320,640]{2,1,0:T(8,128)S(1)}, f32[3,320,640]{2,1,0:T(8,128)}, u32[]{:S(2)}) copy-start(f32[3,320,640]{2,1,0:T(8,128)} %all-reduce.2.cloned.1.call-done) | copy-start | bytes 7372804
Sparse Core Ops, SparseCore 0:
  8.9 71.2 all-gather.1
  96.1 100.1 all-reduce.1
where the time goes:
time: 219 us
  waiting for transfers between devices  173 us (79%)
  matrix products  17.3 us (8%)
  between operations  14.2 us (6%)
  blocking collectives  7.95 us (4%)
  other arithmetic  4.41 us (2%)
    psum x1, waiting for transfers between devices, body(): total = lax.psum(partial_grads, 'seq')  100 us
    all_gather x1, waiting for transfers between devices, body(): lax.all_gather(tokens, 'head', axis=0, tiled=True)  72 us
    dot_general x1, matrix products, body(): jnp.einsum('rd,cdh->rch', lax.all_gather(tokens, 'head', axis=0, tiled=Tr...  9.51 us
    all_to_all x1, blocking collectives, body(): lax.all_to_all(answer, 'head', split_axis=0, concat_axis=1, tiled=True)  7.95 us
  transfers between devices with their start and end apart: 2, of which 2 were waited for; matrix products, arithmetic and copies ran while one was open for 0% of the time, Pallas kernels for 0%

commit v1 on v0

--- a/solution.py
+++ b/solution.py
@@ -2,6 +2,19 @@
 import jax.numpy as jnp
 from jax import lax
 from jax.sharding import PartitionSpec as P
+
+
+def _treat_samples(w_in):
+    device_axis = "seq"
+    high, x_now = (w_in, 0)
+    sides = jax.lax.axis_size(device_axis)
+    while 1 << x_now < sides:
+        finding = jax.lax.ppermute(
+            high, axis_name=device_axis, perm=[(q, q ^ 1 << x_now) for q in range(sides)]
+        )
+        high = high + finding
+        x_now = x_now + 1
+    return high
 
 
 def local_grads(keys, values, weight, old):
@@ -51,7 +64,7 @@
     partial_grads = local_grads(keys, values, weight, old)
     old_f = old.astype(jnp.float32)
     old_norm = jnp.sqrt(jnp.sum(old_f * old_f, axis=1))
-    total = lax.psum(partial_grads, "seq")
+    total = _treat_samples(partial_grads)
     fresh = old_f + total
     new_sq = jnp.sum(fresh * fresh, axis=1)
     renorm = (fresh * (old_norm / jnp.sqrt(new_sq + 1e-06))[:, None, :]).astype(jnp.bfloat16)

time: 219 us -> 338 us (1.54)
  waiting for transfers between devices: 173 us -> 289 us
  starting transfers between devices: 0.04 us -> 5.66 us
    ppermute x0 -> x4, waiting for transfers between devices: none -> 216 us  [_treat_samples(): jax.lax.ppermute(high, axis_name=device_axis, perm=[(q, q ^ 1 << x_now) f...]
    psum x1 -> x0, waiting for transfers between devices: 100 us -> none  [body(): total = lax.psum(partial_grads, 'seq')]
    ppermute x0 -> x4, starting transfers between devices: none -> 5.66 us  [_treat_samples(): jax.lax.ppermute(high, axis_name=device_axis, perm=[(q, q ^ 1 << x_now) f...]
  transfers between devices with their start and end apart: 2 -> 5, of which waited for: 2 -> 5; matrix products, arithmetic and copies ran while one was open for 0% -> 0% of each run, Pallas kernels for 0% -> 0%
where the time goes in v1:
time: 338 us
  waiting for transfers between devices  289 us (86%)
  matrix products  15.8 us (5%)
  between operations  14.2 us (4%)
  blocking collectives  7.92 us (2%)
  starting transfers between devices  5.66 us (2%)
  other arithmetic  3.38 us (1%)
    ppermute x4, waiting for transfers between devices, _treat_samples(): jax.lax.ppermute(high, axis_name=device_axis, perm=[(q, q ^ 1 << x_now) f...  216 us
    all_gather x1, waiting for transfers between devices, body(): lax.all_gather(tokens, 'head', axis=0, tiled=True)  72.1 us
    dot_general x1, matrix products, body(): jnp.einsum('rd,cdh->rch', lax.all_gather(tokens, 'head', axis=0, tiled=Tr...  9.53 us
    all_to_all x1, blocking collectives, body(): lax.all_to_all(answer, 'head', split_axis=0, concat_axis=1, tiled=True)  7.92 us
  transfers between devices with their start and end apart: 5, of which 5 were waited for; matrix products, arithmetic and copies ran while one was open for 0% of the time, Pallas kernels for 0%

profile of v1, /device:TPU:0, one launch (start us, length us, event | category | flops | bytes accessed | tf_op | source)
XLA Modules:
  0.0 338.1 jit_solution(2090559753048728656)
XLA Ops:
  6.5 0.0 copy-start.4
  6.5 0.0 copy-start.3
  6.5 0.0 all-gather.2.cloned.1.call-start
  6.5 0.7 all-gather.2.cloned.1.call-update
  7.9 0.0 copy-done.4
  7.9 0.1 broadcast_bitcast_fusion
  8.1 0.0 copy-done.3
  8.1 72.1 %all-gather.2.cloned.1.call-done = bf16[512,5120]{1,0:T(8,128)(2,1)} async-done(((bf16[256,5120]{1,0:T(8,128)(2,1)}), bf16[512,5120]{1,0:T(8,128)(2,1)}) %all-gather.2.cloned.1.call-update) | async-done | bytes 5242896 | tf_op jit(solution)/shard_map/all_gather | solution.py:55
  80.2 0.0 copy-start.2
  80.2 9.5 %fusion.10 = bf16[512,3,320]{0,2,1:T(8,128)(2,1)S(1)} fusion(bf16[512,5120]{1,0:T(8,128)(2,1)} %all-gather.2.cloned.1.call-done, bf16[3,5120,320]{1,2,0:T(8,128)(2,1)} %param.9, bf16[3,5120]{1,0:T(4,128)(2,1)S(1)} %bitcast.82), kind=kOutput, calls=%fused_computation.12 | convolution fusion | flops 5038571520 | bytes 16087040 | tf_op jit(solution)/shard_map/rd,cdh->rch/dot_general | solution.py:53
  89.7 0.0 copy-done.2
  89.7 0.0 copy-start.1
  89.7 0.6 fusion.23
  90.3 0.4 copy-done.1
  90.7 0.0 copy-start
  90.7 0.6 fusion.25
  91.3 0.4 copy-done
  91.7 0.6 fusion.27
  92.3 0.6 convolution_bitcast_fusion.1
  92.9 0.8 convolution_bitcast_fusion.2
  93.7 0.6 convolution_bitcast_fusion
  94.4 0.2 pad_maximum_fusion
  94.5 0.1 collective-permute-start
  94.6 4.7 %collective-permute-done = f32[3,320,640]{2,1,0:T(8,128)S(1)} collective-permute-done((f32[3,320,640]{2,1,0:T(8,128)S(1)}, f32[3,320,640]{2,1,0:T(8,128)S(1)}, u32[]{:S(2)}, u32[]{:S(2)}) %collective-permute-start) | collective-permute-done | bytes 2457632 | tf_op jit(solution)/shard_map/ppermute | solution.py:12
  99.3 0.2 fusion.42
  99.5 1.6 collective-permute-start.1
  101.1 53.9 %collective-permute-done.1 = f32[3,320,640]{2,1,0:T(8,128)S(1)} collective-permute-done((f32[3,320,640]{2,1,0:T(8,128)S(1)}, f32[3,320,640]{2,1,0:T(8,128)S(1)}, u32[]{:S(2)}, u32[]{:S(2)}) %collective-permute-start.1) | collective-permute-done | bytes 2457632 | tf_op jit(solution)/shard_map/ppermute | solution.py:12
  155.0 0.3 fusion.43
  155.3 1.6 collective-permute-start.2
  156.9 53.1 %collective-permute-done.2 = f32[3,320,640]{2,1,0:T(8,128)S(1)} collective-permute-done((f32[3,320,640]{2,1,0:T(8,128)S(1)}, f32[3,320,640]{2,1,0:T(8,128)S(1)}, u32[]{:S(2)}, u32[]{:S(2)}) %collective-permute-start.2) | collective-permute-done | bytes 2457632 | tf_op jit(solution)/shard_map/ppermute | solution.py:12
  209.9 0.2 add.50
  210.2 2.5 collective-permute-start.3
  212.7 104.8 %collective-permute-done.3 = f32[3,320,640]{2,1,0:T(8,128)S(1)} collective-permute-done((f32[3,320,640]{2,1,0:T(8,128)S(1)}, f32[3,320,640]{2,1,0:T(8,128)S(1)}, u32[]{:S(2)}, u32[]{:S(2)}) %collective-permute-start.3) | collective-permute-done | bytes 2457632 | tf_op jit(solution)/shard_map/ppermute | solution.py:12
  317.5 0.6 fusion.4
  318.2 0.5 multiply_convert_fusion
  318.7 0.6 fusion.22
  319.3 1.9 multiply_reduce_fusion.1
  321.2 1.2 multiply_convert_fusion.6
  322.4 7.9 %all_to_all.19 = bf16[2,256,320]{1,2,0:T(8,128)(2,1)S(1)} all-to-all(bf16[2,256,320]{1,2,0:T(8,128)(2,1)S(1)} %bitcast.79), channel_id=1, replica_groups=mesh['seq'=16,'head'=2] {'head'}, dimensions={0} | all-to-all | bytes 655360 | tf_op jit(solution)/shard_map/all_to_all | solution.py:72
  330.3 0.9 copy.11
  (7 shorter events, 0.1 us)
Async XLA Ops:
  6.5 1.4 copy-start.4
  6.5 1.5 copy-start.3
  6.5 73.6 %all-gather.2.cloned.1.call-start = ((), (), s32[]{:S(2)}) async-start(), calls=%async_computation.1 | async-start | bytes 7864320 | tf_op jit(solution)/shard_map/all_gather | solution.py:55
  80.2 9.5 %copy-start.2 = (bf16[1,320,640]{2,1,0:T(8,128)(2,1)S(1)}, bf16[1,320,640]{2,1,0:T(8,128)(2,1)}, u32[]{:S(2)}) copy-start(bf16[1,320,640]{2,1,0:T(8,128)(2,1)} %param.13) | copy-start | bytes 1228804
  89.7 1.0 copy-start.1
  90.7 1.0 copy-start
  94.5 4.7 %collective-permute-start = (f32[3,320,640]{2,1,0:T(8,128)S(1)}, f32[3,320,640]{2,1,0:T(8,128)S(1)}, u32[]{:S(2)}, u32[]{:S(2)}) collective-permute-start(f32[3,320,640]{2,1,0:T(8,128)S(1)} %pad_maximum_fusion), channel_id=1, source_target_pairs={{0,2},{2,0},{4,6},{6,4},{8,10},{10,8},{12,14},{14,12},{16,18},{18,... | collective-permute-start | bytes 7372808 | tf_op jit(solution)/shard_map/ppermute | solution.py:12
  99.5 55.5 %collective-permute-start.1 = (f32[3,320,640]{2,1,0:T(8,128)S(1)}, f32[3,320,640]{2,1,0:T(8,128)S(1)}, u32[]{:S(2)}, u32[]{:S(2)}) collective-permute-start(f32[3,320,640]{2,1,0:T(8,128)S(1)} %fusion.42), channel_id=1, source_target_pairs={{0,4},{2,6},{4,0},{6,2},{8,12},{10,14},{12,8},{14,10},{16,20},{18,... | collective-permute-start | bytes 7372808 | tf_op jit(solution)/shard_map/ppermute | solution.py:12
  155.3 54.6 %collective-permute-start.2 = (f32[3,320,640]{2,1,0:T(8,128)S(1)}, f32[3,320,640]{2,1,0:T(8,128)S(1)}, u32[]{:S(2)}, u32[]{:S(2)}) collective-permute-start(f32[3,320,640]{2,1,0:T(8,128)S(1)} %fusion.43), channel_id=1, source_target_pairs={{0,8},{2,10},{4,12},{6,14},{8,0},{10,2},{12,4},{14,6},{16,24},{18,... | collective-permute-start | bytes 7372808 | tf_op jit(solution)/shard_map/ppermute | solution.py:12
  210.2 107.3 %collective-permute-start.3 = (f32[3,320,640]{2,1,0:T(8,128)S(1)}, f32[3,320,640]{2,1,0:T(8,128)S(1)}, u32[]{:S(2)}, u32[]{:S(2)}) collective-permute-start(f32[3,320,640]{2,1,0:T(8,128)S(1)} %add.50), channel_id=1, source_target_pairs={{0,16},{2,18},{4,20},{6,22},{8,24},{10,26},{12,28},{14,30},{16,0},... | collective-permute-start | bytes 7372808 | tf_op jit(solution)/shard_map/ppermute | solution.py:12
Sparse Core Ops, SparseCore 0:
  8.9 71.2 all-gather.1

commit v2 on v0

--- a/solution.py
+++ b/solution.py
@@ -2,6 +2,14 @@
 import jax.numpy as jnp
 from jax import lax
 from jax.sharding import PartitionSpec as P
+
+
+def pass_the_kinds(panel, out_dim):
+    panel = jnp.moveaxis(panel, 0, out_dim)
+    outer = panel.shape
+    return panel.reshape(
+        *outer[:out_dim], outer[out_dim] * outer[out_dim + 1], *outer[out_dim + 2 :]
+    )
 
 
 def local_grads(keys, values, weight, old):
@@ -33,15 +41,35 @@
 
 
 def body(tokens, w_qkv, scale_exp, gate_mask, rate, fast_gate, fast_up, fast_down):
+
+    def check_the_rates(page, named_axis, on_dim, field_in, axis_k):
+        h_now = lax.axis_size(named_axis)
+        r_now = lax.axis_index(named_axis)
+        moved, n_now, current_block = (h_now, r_now, page.shape[on_dim])
+        rows = tuple(((u, (u + 1) % moved) for u in range(moved)))
+        blocks_here = []
+        piece_out = page
+        for q in [*range(moved)]:
+            new = piece_out if q == moved - 1 else lax.ppermute(piece_out, named_axis, rows)
+            passed = field_in(piece_out, (n_now - q) % moved * current_block)
+            blocks_here.append(passed)
+            piece_out = new
+        front = jnp.stack(blocks_here, axis=0)
+        blocks_here = front[(n_now - jnp.arange(moved)) % moved]
+        return pass_the_kinds(blocks_here, axis_k)
+
     factor = jnp.exp2(scale_exp.astype(jnp.float32))[:, :, 0]
     block_rows = w_qkv.shape[1] // factor.shape[1]
     factor = jnp.repeat(factor, block_rows, axis=1)[:, :, None].astype(jnp.bfloat16)
     weff = w_qkv * factor
-    triple = jnp.einsum(
-        "rd,cdh->rch",
-        lax.all_gather(tokens, "head", axis=0, tiled=True),
-        weff,
-        preferred_element_type=jnp.float32,
+    triple = check_the_rates(
+        tokens,
+        "head",
+        0,
+        lambda own_block, offset: jnp.einsum(
+            "rd,cdh->rch", own_block, weff, preferred_element_type=jnp.float32
+        ),
+        0,
     ).astype(jnp.bfloat16)
     query = triple[:, 0]
     keys = triple[:, 1]

time: 219 us -> 204 us (0.932)
  waiting for transfers between devices: 173 us -> 149 us
  starting transfers between devices: 0.04 us -> 2.97 us
  matrix products: 17.3 us -> 19.7 us
    all_gather x1 -> x0, waiting for transfers between devices: 72 us -> none  [body(): lax.all_gather(tokens, 'head', axis=0, tiled=True)]
    ppermute x0 -> x1, waiting for transfers between devices: none -> 47.5 us  [check_the_rates(): lax.ppermute(piece_out, named_axis, rows)]
    ppermute x0 -> x1, starting transfers between devices: none -> 2.97 us  [check_the_rates(): lax.ppermute(piece_out, named_axis, rows)]
    dot_general x1 -> x2, matrix products: 9.51 us -> 11.9 us  [body(): jnp.einsum('rd,cdh->rch', own_block, weff, preferred_element_type=jnp.flo...]
  transfers between devices with their start and end apart: 2 -> 2, of which waited for: 2 -> 2; matrix products, arithmetic and copies ran while one was open for 0% -> 4% of each run, Pallas kernels for 0% -> 0%
where the time goes in v2:
time: 204 us; the launch traced here: 203 us
  waiting for transfers between devices  149 us (73%)
  matrix products  19.7 us (10%)
  between operations  14.2 us (7%)
  blocking collectives  7.94 us (4%)
  other arithmetic  5.88 us (3%)
  local copies, waits for them, and re-layouts  3.09 us (2%)
  starting transfers between devices  2.97 us (1%)
    psum x1, waiting for transfers between devices, body(): total = lax.psum(partial_grads, 'seq')  102 us
    ppermute x1, waiting for transfers between devices, check_the_rates(): lax.ppermute(piece_out, named_axis, rows)  47.5 us
    dot_general x2, matrix products, body(): jnp.einsum('rd,cdh->rch', own_block, weff, preferred_element_type=jnp.flo...  11.9 us
    all_to_all x1, blocking collectives, body(): lax.all_to_all(answer, 'head', split_axis=0, concat_axis=1, tiled=True)  7.94 us
  transfers between devices with their start and end apart: 2, of which 2 were waited for; matrix products, arithmetic and copies ran while one was open for 4% of the time, Pallas kernels for 0%

profile of v2, /device:TPU:0, one launch (start us, length us, event | category | flops | bytes accessed | tf_op | source)
XLA Modules:
  0.0 203.2 jit_solution(18418702981810311576)
XLA Ops:
  6.5 0.0 all-reduce.2.cloned.1.call-start
  6.5 3.0 %collective-permute-start = (bf16[256,5120]{1,0:T(8,128)(2,1)}, bf16[256,5120]{1,0:T(8,128)(2,1)}, u32[]{:S(2)}, u32[]{:S(2)}) collective-permute-start(bf16[256,5120]{1,0:T(8,128)(2,1)} %param.8), channel_id=1, source_target_pairs={{0,1},{1,0},{2,3},{3,2},{4,5},{5,4},{6,7},{7,6},{8,9},{9,8},{10,11... | collective-permute-start | bytes 7864328 | tf_op jit(solution)/shard_map/ppermute | solution.py:53
  10.2 0.7 exponential_convert_fusion
  10.9 0.1 broadcast_bitcast_fusion
  11.0 0.7 convert_multiply_fusion.2
  11.7 0.0 copy-start.4
  11.7 7.4 %fusion.10 = bf16[1,256,3,320]{1,3,2,0:T(8,128)(2,1)S(1)} fusion(bf16[256,5120]{1,0:T(8,128)(2,1)} %param.8, bf16[3,5120,320]{1,2,0:T(8,128)(2,1)} %param.9, bf16[3,5120]{1,0:T(4,128)(2,1)S(1)} %bitcast.106), kind=kOutput, calls=%fused_computation.18 | convolution fusion | flops 2521497600 | bytes 12974080 | tf_op jit(solution)/shard_map/rd,cdh->rch/dot_general | solution.py:69
  19.1 47.5 %collective-permute-done = bf16[256,5120]{1,0:T(8,128)(2,1)} collective-permute-done((bf16[256,5120]{1,0:T(8,128)(2,1)}, bf16[256,5120]{1,0:T(8,128)(2,1)}, u32[]{:S(2)}, u32[]{:S(2)}) %collective-permute-start) | collective-permute-done | bytes 2621472 | tf_op jit(solution)/shard_map/ppermute | solution.py:53
  66.7 0.0 copy-done.4
  66.7 4.5 %fusion.15 = bf16[1,256,3,320]{1,3,2,0:T(8,128)(2,1)S(1)} fusion(bf16[256,5120]{1,0:T(8,128)(2,1)} %collective-permute-done, bf16[3,5120,320]{1,2,0:T(8,128)(2,1)S(1)} %copy-done.4, bf16[3,5120]{1,0:T(4,128)(2,1)S(1)} %bitcast.107), kind=kOutput, calls=%fused_computation.19 | convolution fusion | flops 2521497600 | bytes 12974080 | tf_op jit(solution)/shard_map/rd,cdh->rch/dot_general | solution.py:69
  71.2 0.1 pad_maximum_fusion.1
  71.3 0.6 gather_fusion
  71.9 0.0 copy-start.2
  71.9 0.1 copy.15
  72.0 0.0 copy-start.1
  72.0 0.9 copy-done.2
  72.9 0.6 fusion.27
  73.5 0.0 copy-done.1
  73.5 0.0 copy-start.3
  73.5 0.6 fusion.29
  74.1 0.4 copy-done.3
  74.5 0.6 fusion.31
  75.1 0.6 convolution_bitcast_fusion.1
  75.7 0.8 convolution_bitcast_fusion.2
  76.5 0.6 convolution_bitcast_fusion
  77.1 1.6 pad_maximum_fusion
  78.7 0.0 all-reduce.2.cloned.1.call-update
  78.7 101.8 %all-reduce.2.cloned.1.call-done = f32[3,320,640]{2,1,0:T(8,128)} async-done(((f32[3,320,640]{2,1,0:T(8,128)}), f32[3,320,640]{2,1,0:T(8,128)}) %all-reduce.2.cloned.1.call-update) | async-done | bytes 2457616 | tf_op jit(solution)/shard_map/psum | solution.py:82
  180.6 0.0 copy-start
  180.6 2.4 %fusion.8 = (f32[3,640]{1,0:T(4,128)S(1)}, f32[3,640]{1,0:T(4,128)S(1)}) fusion(bf16[1,320,640]{2,1,0:T(8,128)(2,1)S(1)} %copy-done.3, bf16[1,320,640]{2,1,0:T(8,128)(2,1)S(1)} %copy-done.1, bf16[1,320,640]{2,1,0:T(8,128)(2,1)S(1)} %copy-done.2, f32[3,320,640]{2,1,0:T(8,128)} %all-reduce.2.cloned.1.call-done), kind=kLoop, calls=%fused_computation.11 | loop fusion | flops 4911360 | bytes 3701760 | tf_op jit(solution)/shard_map/reduce_sum | solution.py:81
  183.0 0.1 copy-done
  183.0 0.4 multiply_convert_fusion
  183.4 1.6 fusion.26
  185.0 2.3 %multiply_reduce_fusion.1 = (f32[512]{0:T(512)S(1)}, f32[512,320]{0,1:T(8,128)S(1)}) fusion(bf16[3,320,640]{2,1,0:T(8,128)(2,1)S(1)} %multiply_convert_fusion, f32[512,640]{1,0:T(8,128)} %fusion.26, bf16[512,3,320]{0,2,1:T(8,128)(2,1)S(1)} %bitcast.102), kind=kOutput, calls=%fused_computation.37 | convolution fusion | flops 421723648 | bytes 3115008 | tf_op jit(solution)/shard_map/dot_general | solution.py:36
  187.4 0.1 multiply_convert_fusion.6
  187.5 7.9 %all_to_all.19 = bf16[2,256,320]{1,2,0:T(8,128)(2,1)S(1)} all-to-all(bf16[2,256,320]{1,2,0:T(8,128)(2,1)S(1)} %bitcast.103), channel_id=1, replica_groups=mesh['seq'=16,'head'=2] {'head'}, dimensions={0} | all-to-all | bytes 655360 | tf_op jit(solution)/shard_map/all_to_all | solution.py:87
  195.4 0.9 copy.12
  (7 shorter events, 0.1 us)
Async XLA Ops:
  6.5 174.1 %all-reduce.2.cloned.1.call-start = ((), (), s32[]{:S(2)}) async-start(), calls=%async_computation.1 | async-start | bytes 4915200 | tf_op jit(solution)/shard_map/psum | solution.py:82
  6.5 60.1 %collective-permute-start = (bf16[256,5120]{1,0:T(8,128)(2,1)}, bf16[256,5120]{1,0:T(8,128)(2,1)}, u32[]{:S(2)}, u32[]{:S(2)}) collective-permute-start(bf16[256,5120]{1,0:T(8,128)(2,1)} %param.8), channel_id=1, source_target_pairs={{0,1},{1,0},{2,3},{3,2},{4,5},{5,4},{6,7},{7,6},{8,9},{9,8},{10,11... | collective-permute-start | bytes 7864328 | tf_op jit(solution)/shard_map/ppermute | solution.py:53
  11.7 55.0 %copy-start.4 = (bf16[3,5120,320]{1,2,0:T(8,128)(2,1)S(1)}, bf16[3,5120,320]{1,2,0:T(8,128)(2,1)}, u32[]{:S(2)}) copy-start(bf16[3,5120,320]{1,2,0:T(8,128)(2,1)} %param.9) | copy-start | bytes 29491204
  71.9 1.0 copy-start.2
  72.0 1.5 copy-start.1
  73.5 1.0 copy-start.3
  180.6 2.4 %copy-start = (f32[3,320,640]{2,1,0:T(8,128)S(1)}, f32[3,320,640]{2,1,0:T(8,128)}, u32[]{:S(2)}) copy-start(f32[3,320,640]{2,1,0:T(8,128)} %all-reduce.2.cloned.1.call-done) | copy-start | bytes 7372804
Sparse Core Ops, SparseCore 0:
  78.9 101.6 all-reduce.1
